TPU v7x, 128 devices: a whole 4x4x4 slice. The times are simulated.
128 devices in a mesh: rep: 16 (over y, z), tp: 8 (over x, core).
Axes of the slice: x: 4, y: 4, z: 4, core: 2. Of those that a mesh axis runs over, the one named last changes fastest.
Arguments:
- grads: bfloat16 [16, 12, 768, 2048], P('rep', None, None, 'tp'), may hold values from -6 to 6
- error: float32 [16, 12, 768, 2048], P('rep', None, None, 'tp'), may hold values from -2 to 2
- query: float32 [12, 32, 2048], P(None, None, 'tp'), may hold values from -6 to 6
- momentum: float32 [9216, 2048], P(('rep', 'tp')), may hold values from -0.8 to 0.8
- master: float32 [9216, 2048], P(('rep', 'tp')), may hold values from -0.8 to 0.8
Outputs:
- new_error: float32 [16, 12, 768, 2048], P('rep', None, None, 'tp')
- new_query: float32 [12, 32, 2048], P(None, None, 'tp')
- new_momentum: float32 [9216, 2048], P(('rep', 'tp'))
- new_master: float32 [9216, 2048], P(('rep', 'tp'))
- weights: bfloat16 [12, 768, 2048], P(None, None, 'tp')
All inputs are finite; a program needn't handle non-finite values.
Results may differ from a plain program's by a relative error of at most 0.0004.
Values may be sent and summed in bfloat16 or wider, within the bound.
A program may use at most 128 MiB of HBM per device.

v0:
```python
import jax
import jax.numpy as jnp
from jax import lax
from jax.sharding import PartitionSpec as P

ROUNDS = 2
NS_STEPS = 5
NORM_EPSILON = 1e-06
MOMENTUM_DECAY = 0.9
LEARNING_RATE = 0.5


def local_gram(factor):
    return jnp.einsum("krd,ksd->krs", factor, factor, precision=lax.Precision.HIGHEST)


def orthonormal(factor, gram_of):
    gram_now = gram_of(factor)
    sum_squares = jnp.trace(gram_now, axis1=1, axis2=2)[:, None, None]
    factor_scale = lax.rsqrt(sum_squares + NORM_EPSILON)
    ortho_basis = factor * factor_scale
    gram_now = gram_now * (factor_scale * factor_scale)
    for iteration in range(NS_STEPS):
        if iteration > 0:
            gram_now = gram_of(ortho_basis)
        ortho_basis = 1.5 * ortho_basis - 0.5 * jnp.einsum(
            "krs,ksd->krd", gram_now, ortho_basis, precision=lax.Precision.HIGHEST
        )
    return ortho_basis


def local(grads, error, query, momentum, master):
    corrected = grads[0].astype(jnp.float32) + error[0]
    current = query
    replicas = lax.axis_size("rep")
    for power_pass in range(ROUNDS):
        partial_factor = jnp.einsum(
            "kdf,krf->krd", corrected, current, precision=lax.Precision.HIGHEST
        )
        summed = lax.psum(partial_factor, ("rep", "tp"))
        ortho_basis = orthonormal(summed, local_gram)
        partial_query = jnp.einsum(
            "kdf,krd->krf", corrected, ortho_basis, precision=lax.Precision.HIGHEST
        )
        current = lax.psum(partial_query, "rep") / replicas
    approx = jnp.einsum("krd,krf->kdf", ortho_basis, current, precision=lax.Precision.HIGHEST)
    new_error = (corrected - approx)[None]
    matrices, model_width, shard_cols = approx.shape
    block_rows = matrices * model_width // replicas
    approx_rows = approx.reshape(matrices * model_width, shard_cols)
    own_block = lax.dynamic_slice_in_dim(
        approx_rows, lax.axis_index("rep") * block_rows, block_rows, 0
    )
    flat_approx = lax.all_to_all(own_block, "tp", split_axis=0, concat_axis=1, tiled=True)
    new_momentum = MOMENTUM_DECAY * momentum + flat_approx
    new_master = master - LEARNING_RATE * new_momentum
    working = new_master.astype(jnp.bfloat16)
    by_columns = lax.all_to_all(working, "tp", split_axis=1, concat_axis=0, tiled=True)
    weight_rows = lax.all_gather(by_columns, "rep", axis=0, tiled=True)
    weights = weight_rows.reshape(matrices, model_width, shard_cols)
    return (new_error, current, new_momentum, new_master, weights)


def solution(mesh):
    placed = (
        P("rep", None, None, "tp"),
        P("rep", None, None, "tp"),
        P(None, None, "tp"),
        P(("rep", "tp"), None),
        P(("rep", "tp"), None),
    )
    return jax.shard_map(
        local,
        mesh=mesh,
        in_specs=placed,
        out_specs=(
            P("rep", None, None, "tp"),
            P(None, None, "tp"),
            P(("rep", "tp"), None),
            P(("rep", "tp"), None),
            P(None, None, "tp"),
        ),
        check_vma=False,
    )
```

profile of v0, /device:TPU:1, one launch (start us, length us, event | category | flops | bytes accessed | tf_op | source)
XLA Modules:
  0.0 643.5 jit_solution(3805032442626660912)
XLA Ops:
  7.2 0.0 all-reduce.5.cloned.1.call-start
  7.2 0.9 copy-done
  8.2 14.9 %fusion.9 = f32[12,32,768]{2,1,0:T(8,128)} fusion(f32[12,32,256]{2,1,0:T(8,128)S(1)} %copy-done, f32[1,12,768,256]{3,2,1,0:T(8,128)} %param.6, bf16[1,12,768,256]{3,2,1,0:T(8,128)(2,1)} %param.5), kind=kOutput, calls=%fused_computation.11 | convolution fusion | flops 910688256 | bytes 15728640 | tf_op jit(solution)/shard_map/kdf,krf->krd/dot_general | solution.py:37
  23.1 0.0 all-reduce.5.cloned.1.call-update
  23.1 0.2 all-reduce.7.cloned.1.call-start
  23.3 150.7 %all-reduce.5.cloned.1.call-done = f32[12,32,768]{2,1,0:T(8,128)} async-done(((f32[12,32,768]{2,1,0:T(8,128)}), f32[12,32,768]{2,1,0:T(8,128)}) %all-reduce.5.cloned.1.call-update) | async-done | bytes 1179664 | tf_op jit(solution)/shard_map/psum | solution.py:40
  174.1 3.0 select_reduce_fusion.1
  177.1 1.3 fusion.21
  178.4 1.2 fusion.36
  179.6 1.2 fusion.20
  180.9 1.2 fusion.37
  182.1 1.2 fusion.19
  183.3 1.2 fusion.38
  184.5 1.2 fusion.18
  185.7 1.2 fusion.39
  186.9 1.2 fusion.17
  188.1 0.4 slice-done.6
  188.6 6.7 %fusion.4 = f32[12,32,256]{2,1,0:T(8,128)} fusion(f32[12,32,768]{2,1,0:T(8,128)S(1)} %fusion.17, f32[1,12,768,256]{3,2,1,0:T(8,128)S(1)} %bitcast.73, bf16[1,12,768,256]{3,2,1,0:T(8,128)(2,1)S(1)} %bitcast.77), kind=kOutput, calls=%fused_computation.5 | convolution fusion | flops 910688256 | bytes 15728640 | tf_op jit(solution)/shard_map/kdf,krd->krf/dot_general | solution.py:42
  195.3 0.0 all-reduce.7.cloned.1.call-update
  195.3 0.0 all-reduce.9.cloned.1.call-start
  195.4 81.4 %all-reduce.7.cloned.1.call-done = f32[12,32,256]{2,1,0:T(8,128)} async-done(((f32[12,32,256]{2,1,0:T(8,128)}), f32[12,32,256]{2,1,0:T(8,128)}) %all-reduce.7.cloned.1.call-update) | async-done | bytes 393232 | tf_op jit(solution)/shard_map/psum | solution.py:45
  276.8 14.6 %fusion.2 = f32[12,32,768]{2,1,0:T(8,128)} fusion(f32[12,32,256]{2,1,0:T(8,128)} %all-reduce.7.cloned.1.call-done, f32[1,12,768,256]{3,2,1,0:T(8,128)} %param.6, bf16[1,12,768,256]{3,2,1,0:T(8,128)(2,1)} %param.5), kind=kOutput, calls=%fused_computation.3 | convolution fusion | flops 910786560 | bytes 15728640 | tf_op jit(solution)/shard_map/kdf,krf->krd/dot_general | solution.py:37
  291.3 0.0 all-reduce.9.cloned.1.call-update
  291.4 0.2 all-reduce.11.cloned.1.call-start
  291.6 148.1 %all-reduce.9.cloned.1.call-done = f32[12,32,768]{2,1,0:T(8,128)} async-done(((f32[12,32,768]{2,1,0:T(8,128)}), f32[12,32,768]{2,1,0:T(8,128)}) %all-reduce.9.cloned.1.call-update) | async-done | bytes 1179664 | tf_op jit(solution)/shard_map/psum | solution.py:40
  439.7 3.0 select_reduce_fusion
  442.7 1.3 fusion.16
  444.0 1.2 fusion.40
  445.3 1.2 fusion.15
  446.5 1.2 fusion.41
  447.7 1.2 fusion.14
  448.9 1.2 fusion.42
  450.1 1.2 fusion.13
  451.3 1.2 fusion.43
  452.5 1.2 fusion.12
  454.0 6.8 %fusion = f32[12,32,256]{2,1,0:T(8,128)} fusion(f32[12,32,768]{2,1,0:T(8,128)S(1)} %fusion.12, f32[1,12,768,256]{3,2,1,0:T(8,128)S(1)} %bitcast.75, bf16[1,12,768,256]{3,2,1,0:T(8,128)(2,1)S(1)} %bitcast.79), kind=kOutput, calls=%fused_computation.1 | convolution fusion | flops 910688256 | bytes 15728640 | tf_op jit(solution)/shard_map/kdf,krd->krf/dot_general | solution.py:42
  460.7 0.0 all-reduce.11.cloned.1.call-update
  460.8 0.0 all-gather.2.cloned.1.call-start
  460.8 81.4 %all-reduce.11.cloned.1.call-done = f32[12,32,256]{2,1,0:T(8,128)} async-done(((f32[12,32,256]{2,1,0:T(8,128)}), f32[12,32,256]{2,1,0:T(8,128)}) %all-reduce.11.cloned.1.call-update) | async-done | bytes 393232 | tf_op jit(solution)/shard_map/psum | solution.py:45
  542.2 1.0 broadcast_multiply_fusion
  543.3 7.7 %fusion.44 = f32[12,768,256]{2,1,0:T(8,128)S(1)} fusion(f32[12,32,768]{2,1,0:T(8,128)S(1)} %fusion.12, f32[12,32,256]{2,1,0:T(8,128)S(1)} %broadcast_multiply_fusion), kind=kOutput, calls=%fused_computation.64 | convolution fusion | flops 905969664 | bytes 11010048 | tf_op jit(solution)/shard_map/krd,krf->kdf/dot_general | solution.py:46
  551.1 16.7 %all_to_all.38 = f32[8,72,256]{2,1,0:T(8,128)S(1)} all-to-all(f32[8,72,256]{2,1,0:T(8,128)S(1)} %bitcast.83), channel_id=1, replica_groups=mesh['rep'=16,'tp'=8] {'tp'}, dimensions={0} | all-to-all | bytes 1179648 | tf_op jit(solution)/shard_map/all_to_all | solution.py:54
  567.9 1.2 fusion.35
  569.1 11.1 %all_to_all.39 = bf16[72,8,256]{2,0,1:T(8,128)(2,1)} all-to-all(bf16[72,8,256]{2,0,1:T(8,128)(2,1)S(1)} %bitcast.87), channel_id=1, replica_groups=mesh['rep'=16,'tp'=8] {'tp'}, dimensions={1} | all-to-all | bytes 589824 | tf_op jit(solution)/shard_map/all_to_all | solution.py:58
  580.2 0.0 all-gather.2.cloned.1.call-update
  580.3 12.7 %fusion.8 = f32[1,12,768,256]{3,2,1,0:T(8,128)} fusion(f32[12,768,256]{2,1,0:T(8,128)} %copy-done.2, f32[1,12,768,256]{3,2,1,0:T(8,128)} %param.6, bf16[1,12,768,256]{3,2,1,0:T(8,128)(2,1)} %param.5), kind=kLoop, calls=%fused_computation.9 | loop fusion | flops 7077888 | bytes 33030144 | tf_op jit(solution)/shard_map/broadcast_in_dim | solution.py:47
  592.9 38.9 %all-gather.2.cloned.1.call-done = bf16[9216,256]{1,0:T(8,128)(2,1)} async-done(((bf16[576,256]{1,0:T(8,128)(2,1)}), bf16[9216,256]{1,0:T(8,128)(2,1)}) %all-gather.2.cloned.1.call-update) | async-done | bytes 4718608 | tf_op jit(solution)/shard_map/all_gather | solution.py:59
  631.8 4.9 copy.24
  (44 shorter events, 0.3 us)
Async XLA Ops:
  7.2 1.0 copy-start
  7.2 166.9 %all-reduce.5.cloned.1.call-start = ((), (), s32[]{:S(2)}) async-start(), calls=%async_computation.2 | async-start | bytes 2359296 | tf_op jit(solution)/shard_map/psum | solution.py:40
  23.1 253.7 %all-reduce.7.cloned.1.call-start = ((), (), s32[]{:S(2)}) async-start(), calls=%async_computation.3 | async-start | bytes 786432 | tf_op jit(solution)/shard_map/psum | solution.py:45
  174.1 3.0 copy-start.3
  178.4 9.7 %slice-start = ((s8[9437184]{0:T(1024)(128)(4,1)}), s8[4194304]{0:T(1024)(128)(4,1)S(1)}, s32[]{:S(2)}) async-start(s8[9437184]{0:T(1024)(128)(4,1)} %bitcast.72), calls=%async_computation.7 | async-start | bytes 8388608
  179.6 8.9 %slice-start.6 = ((s8[4718592]{0:T(1024)(128)(4,1)}), s8[4194304]{0:T(1024)(128)(4,1)S(1)}, s32[]{:S(2)}) async-start(s8[4718592]{0:T(1024)(128)(4,1)} %bitcast.76), calls=%async_computation.13 | async-start | bytes 8388608
  180.9 7.6 %slice-start.1 = ((s8[9437184]{0:T(1024)(128)(4,1)}), s8[4194304]{0:T(1024)(128)(4,1)S(1)}, s32[]{:S(2)}) async-start(s8[9437184]{0:T(1024)(128)(4,1)} %bitcast.72), calls=%async_computation.8 | async-start | bytes 8388608
  183.3 5.3 slice-start.7
  184.5 4.0 slice-start.2
  195.3 244.4 %all-reduce.9.cloned.1.call-start = ((), (), s32[]{:S(2)}) async-start(), calls=%async_computation.4 | async-start | bytes 2359296 | tf_op jit(solution)/shard_map/psum | solution.py:40
  291.4 250.9 %all-reduce.11.cloned.1.call-start = ((), (), s32[]{:S(2)}) async-start(), calls=%async_computation.5 | async-start | bytes 786432 | tf_op jit(solution)/shard_map/psum | solution.py:45
  439.7 3.0 copy-start.4
  444.0 9.7 %slice-start.3 = ((s8[9437184]{0:T(1024)(128)(4,1)}), s8[4194304]{0:T(1024)(128)(4,1)S(1)}, s32[]{:S(2)}) async-start(s8[9437184]{0:T(1024)(128)(4,1)} %bitcast.74), calls=%async_computation.10 | async-start | bytes 8388608
  445.2 8.5 %slice-start.8 = ((s8[4718592]{0:T(1024)(128)(4,1)}), s8[4194304]{0:T(1024)(128)(4,1)S(1)}, s32[]{:S(2)}) async-start(s8[4718592]{0:T(1024)(128)(4,1)} %bitcast.78), calls=%async_computation.15 | async-start | bytes 8388608
  446.5 7.2 %slice-start.4 = ((s8[9437184]{0:T(1024)(128)(4,1)}), s8[4194304]{0:T(1024)(128)(4,1)S(1)}, s32[]{:S(2)}) async-start(s8[9437184]{0:T(1024)(128)(4,1)} %bitcast.74), calls=%async_computation.11 | async-start | bytes 8388608
  448.9 4.8 slice-start.9
  450.1 3.8 slice-start.5
  460.8 171.1 %all-gather.2.cloned.1.call-start = ((), (), s32[]{:S(2)}) async-start(), calls=%async_computation.6 | async-start | bytes 5013504 | tf_op jit(solution)/shard_map/all_gather | solution.py:59
  543.3 7.8 %copy-start.5 = (f32[12,32,256]{2,1,0:T(8,128)}, f32[12,32,256]{2,1,0:T(8,128)S(1)}, u32[]{:S(2)}) copy-start(f32[12,32,256]{2,1,0:T(8,128)S(1)} %broadcast_multiply_fusion) | copy-start | bytes 1179652
  551.0 18.1 %copy-start.2 = (f32[12,768,256]{2,1,0:T(8,128)}, f32[12,768,256]{2,1,0:T(8,128)S(1)}, u32[]{:S(2)}) copy-start(f32[12,768,256]{2,1,0:T(8,128)S(1)} %fusion.44) | copy-start | bytes 28311556
  551.1 16.8 %copy-start.6 = (f32[72,2048]{1,0:T(8,128)S(1)}, f32[72,2048]{1,0:T(8,128)}, u32[]{:S(2)}) copy-start(f32[72,2048]{1,0:T(8,128)} %param.9) | copy-start | bytes 1769476
  551.1 16.8 %copy-start.7 = (f32[72,2048]{1,0:T(8,128)S(1)}, f32[72,2048]{1,0:T(8,128)}, u32[]{:S(2)}) copy-start(f32[72,2048]{1,0:T(8,128)} %param.8) | copy-start | bytes 1769476
  631.8 4.9 copy-start.1
Sparse Core Ops, SparseCore 0:
  23.2 150.8 all-reduce.4
  195.4 81.3 all-reduce.6
  291.5 148.1 all-reduce.8
  460.9 81.3 all-reduce.10
  580.4 51.3 all-gather.1
where the time goes:
time: 649 us; the launch traced here: 643 us
  waiting for transfers between devices  501 us (77%)
  matrix products  78.5 us (12%)
  blocking collectives  27.8 us (4%)
  other arithmetic  14.9 us (2%)
  between operations  14.6 us (2%)
    psum x2, waiting for transfers between devices, local(): summed = lax.psum(partial_factor, ('rep', 'tp'))  299 us
    psum x2, waiting for transfers between devices, local(): current = lax.psum(partial_query, 'rep') / replicas  163 us
    all_gather x1, waiting for transfers between devices, local(): weight_rows = lax.all_gather(by_columns, 'rep', axis=0, tiled=True)  38.9 us
    dot_general x2, matrix products, local(): jnp.einsum('kdf,krf->krd', corrected, current, precision=lax.Precision.HI...  29.5 us
    all_to_all x1, blocking collectives, local(): lax.all_to_all(own_block, 'tp', split_axis=0, concat_axis=1, tiled=True)  16.7 us
    dot_general x10, matrix products, local_gram(): jnp.einsum('krd,ksd->krs', factor, factor, precision=lax.Precision.HIGHEST)  15.7 us
    dot_general x2, matrix products, local(): jnp.einsum('kdf,krd->krf', corrected, ortho_basis, precision=lax.Precisio...  13.5 us
  transfers between devices with their start and end apart: 5, of which 5 were waited for; matrix products, arithmetic and copies ran while one was open for 2% of the time, Pallas kernels for 0%

commit v1 on v0

--- a/solution.py
+++ b/solution.py
@@ -56,7 +56,25 @@
     new_master = master - LEARNING_RATE * new_momentum
     working = new_master.astype(jnp.bfloat16)
     by_columns = lax.all_to_all(working, "tp", split_axis=1, concat_axis=0, tiled=True)
-    weight_rows = lax.all_gather(by_columns, "rep", axis=0, tiled=True)
+    count, index, rows = (lax.axis_size("rep"), lax.axis_index("rep"), by_columns.shape[0])
+    upward = [(i, (i + 1) % count) for i in range(count)]
+    left = [(i, (i - 1) % count) for i in range(count)]
+    weight_rows = jnp.zeros(
+        (*by_columns.shape[:0], count * rows, *by_columns.shape[0 + 1 :]), by_columns.dtype
+    )
+    weight_rows = lax.dynamic_update_slice_in_dim(weight_rows, by_columns, index * rows, axis=0)
+    from_left = from_right = by_columns
+    half = count // 2
+    for step in range(1, half + 1):
+        from_left = lax.ppermute(from_left, "rep", upward)
+        weight_rows = lax.dynamic_update_slice_in_dim(
+            weight_rows, from_left, (index - step) % count * rows, axis=0
+        )
+        if step < count - half:
+            from_right = lax.ppermute(from_right, "rep", left)
+            weight_rows = lax.dynamic_update_slice_in_dim(
+                weight_rows, from_right, (index + step) % count * rows, axis=0
+            )
     weights = weight_rows.reshape(matrices, model_width, shard_cols)
     return (new_error, current, new_momentum, new_master, weights)
 

time: 649 us -> 687 us (1.059); the launches traced: 643 us -> 674 us
  starting transfers between devices: 0.56 us -> 35.4 us
    all_gather x1 -> x0, waiting for transfers between devices: 38.9 us -> none  [local(): weight_rows = lax.all_gather(by_columns, 'rep', axis=0, tiled=True)]
    ppermute x0 -> x15, waiting for transfers between devices: none -> 36.4 us  [the longest x8 36.2 us: local(): from_left = lax.ppermute(from_left, 'rep', upward)]
    ppermute x0 -> x15, starting transfers between devices: none -> 34.8 us  [the longest x7 34 us: local(): from_right = lax.ppermute(from_right, 'rep', left)]
  transfers between devices with their start and end apart: 5 -> 19, of which waited for: 5 -> 12; matrix products, arithmetic and copies ran while one was open for 2% -> 2% of each run, Pallas kernels for 0% -> 0%
where the time goes in v1:
time: 687 us; the launch traced here: 674 us
  waiting for transfers between devices  498 us (72%)
  matrix products  78.9 us (11%)
  starting transfers between devices  35.4 us (5%)
  blocking collectives  27.1 us (4%)
  between operations  15 us (2%)
  other arithmetic  14.7 us (2%)
    psum x2, waiting for transfers between devices, local(): summed = lax.psum(partial_factor, ('rep', 'tp'))  299 us
    psum x2, waiting for transfers between devices, local(): current = lax.psum(partial_query, 'rep') / replicas  163 us
    ppermute x8, waiting for transfers between devices, local(): from_left = lax.ppermute(from_left, 'rep', upward)  36.2 us
    ppermute x7, starting transfers between devices, local(): from_right = lax.ppermute(from_right, 'rep', left)  34 us
    dot_general x2, matrix products, local(): jnp.einsum('kdf,krf->krd', corrected, current, precision=lax.Precision.HI...  29.5 us
    all_to_all x1, blocking collectives, local(): lax.all_to_all(own_block, 'tp', split_axis=0, concat_axis=1, tiled=True)  16.7 us
    dot_general x10, matrix products, local_gram(): jnp.einsum('krd,ksd->krs', factor, factor, precision=lax.Precision.HIGHEST)  15.8 us
  transfers between devices with their start and end apart: 19, of which 12 were waited for; matrix products, arithmetic and copies ran while one was open for 2% of the time, Pallas kernels for 0%

profile of v1, /device:TPU:1, one launch (start us, length us, event | category | flops | bytes accessed | tf_op | source)
XLA Modules:
  0.0 673.9 jit_solution(306003683424765598)
XLA Ops:
  8.2 14.9 %fusion.9 = f32[12,32,768]{2,1,0:T(8,128)} fusion(f32[12,32,256]{2,1,0:T(8,128)S(1)} %copy-done, f32[1,12,768,256]{3,2,1,0:T(8,128)} %param.6, bf16[1,12,768,256]{3,2,1,0:T(8,128)(2,1)} %param.5), kind=kOutput, calls=%fused_computation.11 | convolution fusion | flops 910688256 | bytes 15728640 | tf_op jit(solution)/shard_map/kdf,krf->krd/dot_general | solution.py:37
  23.4 150.7 %all-reduce.5.cloned.1.call-done = f32[12,32,768]{2,1,0:T(8,128)} async-done(((f32[12,32,768]{2,1,0:T(8,128)}), f32[12,32,768]{2,1,0:T(8,128)}) %all-reduce.5.cloned.1.call-update) | async-done | bytes 1179664 | tf_op jit(solution)/shard_map/psum | solution.py:40
  174.1 3.1 select_reduce_fusion.1
  177.2 1.3 fusion.21
  178.5 1.2 fusion.36
  179.8 1.2 fusion.20
  181.0 1.2 fusion.37
  182.2 1.2 fusion.19
  183.4 1.2 fusion.38
  184.6 1.2 fusion.18
  185.8 1.2 fusion.39
  187.0 1.2 fusion.17
  188.7 6.7 fusion.4
  195.5 81.4 %all-reduce.7.cloned.1.call-done = f32[12,32,256]{2,1,0:T(8,128)} async-done(((f32[12,32,256]{2,1,0:T(8,128)}), f32[12,32,256]{2,1,0:T(8,128)}) %all-reduce.7.cloned.1.call-update) | async-done | bytes 393232 | tf_op jit(solution)/shard_map/psum | solution.py:45
  276.9 14.6 %fusion.2 = f32[12,32,768]{2,1,0:T(8,128)} fusion(f32[12,32,256]{2,1,0:T(8,128)} %all-reduce.7.cloned.1.call-done, f32[1,12,768,256]{3,2,1,0:T(8,128)} %param.6, bf16[1,12,768,256]{3,2,1,0:T(8,128)(2,1)} %param.5), kind=kOutput, calls=%fused_computation.3 | convolution fusion | flops 910786560 | bytes 15728640 | tf_op jit(solution)/shard_map/kdf,krf->krd/dot_general | solution.py:37
  291.8 148.1 %all-reduce.9.cloned.1.call-done = f32[12,32,768]{2,1,0:T(8,128)} async-done(((f32[12,32,768]{2,1,0:T(8,128)}), f32[12,32,768]{2,1,0:T(8,128)}) %all-reduce.9.cloned.1.call-update) | async-done | bytes 1179664 | tf_op jit(solution)/shard_map/psum | solution.py:40
  439.9 3.1 select_reduce_fusion
  443.0 1.3 fusion.16
  444.3 1.2 fusion.40
  445.5 1.2 fusion.15
  446.7 1.2 fusion.41
  447.9 1.2 fusion.14
  449.1 1.2 fusion.42
  450.3 1.2 fusion.13
  451.5 1.2 fusion.43
  452.7 1.2 fusion.12
  454.2 6.8 %fusion = f32[12,32,256]{2,1,0:T(8,128)} fusion(f32[12,32,768]{2,1,0:T(8,128)S(1)} %fusion.12, f32[1,12,768,256]{3,2,1,0:T(8,128)S(1)} %bitcast.75, bf16[1,12,768,256]{3,2,1,0:T(8,128)(2,1)S(1)} %bitcast.79), kind=kOutput, calls=%fused_computation.1 | convolution fusion | flops 910688256 | bytes 15728640 | tf_op jit(solution)/shard_map/kdf,krd->krf/dot_general | solution.py:42
  461.0 81.5 %all-reduce.11.cloned.1.call-done = f32[12,32,256]{2,1,0:T(8,128)} async-done(((f32[12,32,256]{2,1,0:T(8,128)}), f32[12,32,256]{2,1,0:T(8,128)}) %all-reduce.11.cloned.1.call-update) | async-done | bytes 393232 | tf_op jit(solution)/shard_map/psum | solution.py:45
  543.5 8.0 %fusion.44 = f32[12,768,256]{2,1,0:T(8,128)S(1)} fusion(f32[12,32,768]{2,1,0:T(8,128)S(1)} %fusion.12, f32[12,32,256]{2,1,0:T(8,128)S(1)} %broadcast_multiply_fusion), kind=kOutput, calls=%fused_computation.80 | convolution fusion | flops 905969664 | bytes 11010048 | tf_op jit(solution)/shard_map/krd,krf->kdf/dot_general | solution.py:46
  551.7 16.7 %all_to_all.38 = f32[8,72,256]{2,1,0:T(8,128)S(1)} all-to-all(f32[8,72,256]{2,1,0:T(8,128)S(1)} %bitcast.84), channel_id=1, replica_groups=mesh['rep'=16,'tp'=8] {'tp'}, dimensions={0} | all-to-all | bytes 1179648 | tf_op jit(solution)/shard_map/all_to_all | solution.py:54
  568.4 1.2 fusion.35
  569.6 10.4 %all_to_all.39 = bf16[72,8,256]{2,0,1:T(8,128)(2,1)S(1)} all-to-all(bf16[72,8,256]{2,0,1:T(8,128)(2,1)S(1)} %bitcast.86), channel_id=1, replica_groups=mesh['rep'=16,'tp'=8] {'tp'}, dimensions={1} | all-to-all | bytes 589824 | tf_op jit(solution)/shard_map/all_to_all | solution.py:58
  580.9 4.0 collective-permute-start.1
  584.9 6.5 collective-permute-done
  591.4 4.8 collective-permute-start.3
  596.2 5.6 collective-permute-done.2
  601.8 4.8 collective-permute-start.5
  606.6 12.5 %fusion.8 = f32[1,12,768,256]{3,2,1,0:T(8,128)} fusion(f32[12,768,256]{2,1,0:T(8,128)} %copy-done.2, f32[1,12,768,256]{3,2,1,0:T(8,128)} %param.6, bf16[1,12,768,256]{3,2,1,0:T(8,128)(2,1)} %param.5), kind=kLoop, calls=%fused_computation.9 | loop fusion | flops 7077888 | bytes 33030144 | tf_op jit(solution)/shard_map/broadcast_in_dim | solution.py:47
  619.5 4.8 collective-permute-start.7
  624.4 3.6 collective-permute-done.6
  628.1 5.2 collective-permute-start.9
  633.3 3.6 collective-permute-done.8
  637.0 5.2 collective-permute-start.11
  642.2 3.6 collective-permute-done.10
  645.9 5.2 collective-permute-start.13
  651.1 3.6 collective-permute-done.12
  655.0 9.7 %collective-permute-done.14 = bf16[576,256]{1,0:T(8,128)(2,1)S(1)} collective-permute-done((bf16[576,256]{1,0:T(8,128)(2,1)S(1)}, bf16[576,256]{1,0:T(8,128)(2,1)S(1)}, u32[]{:S(2)}, u32[]{:S(2)}) %collective-permute-start.14) | collective-permute-done | bytes 294944 | tf_op jit(solution)/shard_map/ppermute | solution.py:69
  664.7 2.2 copy-done.5
  (89 shorter events, 5.1 us)
Async XLA Ops:
  7.2 1.0 copy-start
  7.2 166.9 %all-reduce.5.cloned.1.call-start = ((), (), s32[]{:S(2)}) async-start(), calls=%async_computation.2 | async-start | bytes 2359296 | tf_op jit(solution)/shard_map/psum | solution.py:40
  23.1 253.8 %all-reduce.7.cloned.1.call-start = ((), (), s32[]{:S(2)}) async-start(), calls=%async_computation.3 | async-start | bytes 786432 | tf_op jit(solution)/shard_map/psum | solution.py:45
  174.1 3.1 copy-start.3
  178.5 9.7 %slice-start = ((s8[9437184]{0:T(1024)(128)(4,1)}), s8[4194304]{0:T(1024)(128)(4,1)S(1)}, s32[]{:S(2)}) async-start(s8[9437184]{0:T(1024)(128)(4,1)} %bitcast.72), calls=%async_computation.6 | async-start | bytes 8388608
  179.7 8.9 %slice-start.6 = ((s8[4718592]{0:T(1024)(128)(4,1)}), s8[4194304]{0:T(1024)(128)(4,1)S(1)}, s32[]{:S(2)}) async-start(s8[4718592]{0:T(1024)(128)(4,1)} %bitcast.76), calls=%async_computation.12 | async-start | bytes 8388608
  181.0 7.7 %slice-start.1 = ((s8[9437184]{0:T(1024)(128)(4,1)}), s8[4194304]{0:T(1024)(128)(4,1)S(1)}, s32[]{:S(2)}) async-start(s8[9437184]{0:T(1024)(128)(4,1)} %bitcast.72), calls=%async_computation.7 | async-start | bytes 8388608
  183.4 5.3 slice-start.7
  184.6 4.1 slice-start.2
  195.5 244.4 %all-reduce.9.cloned.1.call-start = ((), (), s32[]{:S(2)}) async-start(), calls=%async_computation.4 | async-start | bytes 2359296 | tf_op jit(solution)/shard_map/psum | solution.py:40
  291.5 251.0 %all-reduce.11.cloned.1.call-start = ((), (), s32[]{:S(2)}) async-start(), calls=%async_computation.5 | async-start | bytes 786432 | tf_op jit(solution)/shard_map/psum | solution.py:45
  439.9 3.1 copy-start.4
  444.3 9.7 %slice-start.3 = ((s8[9437184]{0:T(1024)(128)(4,1)}), s8[4194304]{0:T(1024)(128)(4,1)S(1)}, s32[]{:S(2)}) async-start(s8[9437184]{0:T(1024)(128)(4,1)} %bitcast.74), calls=%async_computation.9 | async-start | bytes 8388608
  445.5 8.5 %slice-start.8 = ((s8[4718592]{0:T(1024)(128)(4,1)}), s8[4194304]{0:T(1024)(128)(4,1)S(1)}, s32[]{:S(2)}) async-start(s8[4718592]{0:T(1024)(128)(4,1)} %bitcast.78), calls=%async_computation.14 | async-start | bytes 8388608
  446.7 7.2 %slice-start.4 = ((s8[9437184]{0:T(1024)(128)(4,1)}), s8[4194304]{0:T(1024)(128)(4,1)S(1)}, s32[]{:S(2)}) async-start(s8[9437184]{0:T(1024)(128)(4,1)} %bitcast.74), calls=%async_computation.10 | async-start | bytes 8388608
  449.1 4.8 slice-start.9
  450.3 3.9 slice-start.5
  543.5 8.0 %copy-start.6 = (f32[12,32,256]{2,1,0:T(8,128)}, f32[12,32,256]{2,1,0:T(8,128)S(1)}, u32[]{:S(2)}) copy-start(f32[12,32,256]{2,1,0:T(8,128)S(1)} %broadcast_multiply_fusion) | copy-start | bytes 1179652
  551.6 18.1 %copy-start.2 = (f32[12,768,256]{2,1,0:T(8,128)}, f32[12,768,256]{2,1,0:T(8,128)S(1)}, u32[]{:S(2)}) copy-start(f32[12,768,256]{2,1,0:T(8,128)S(1)} %fusion.44) | copy-start | bytes 28311556
  551.6 16.8 %copy-start.7 = (f32[72,2048]{1,0:T(8,128)S(1)}, f32[72,2048]{1,0:T(8,128)}, u32[]{:S(2)}) copy-start(f32[72,2048]{1,0:T(8,128)} %param.9) | copy-start | bytes 1769476
  551.6 16.8 %copy-start.8 = (f32[72,2048]{1,0:T(8,128)S(1)}, f32[72,2048]{1,0:T(8,128)}, u32[]{:S(2)}) copy-start(f32[72,2048]{1,0:T(8,128)} %param.8) | copy-start | bytes 1769476
  580.1 11.3 %collective-permute-start = (bf16[576,256]{1,0:T(8,128)(2,1)S(1)}, bf16[576,256]{1,0:T(8,128)(2,1)S(1)}, u32[]{:S(2)}, u32[]{:S(2)}) collective-permute-start(bf16[576,256]{1,0:T(8,128)(2,1)S(1)} %bitcast.87), channel_id=1, source_target_pairs={{0,8},{8,16},{16,24},{24,32},{32,40},{40,48},{48,56},{56,64},{64,7... | collective-permute-start | bytes 884744 | tf_op jit(solution)/shard_map/ppermute | solution.py:69
  580.9 10.5 %collective-permute-start.1 = (bf16[576,256]{1,0:T(8,128)(2,1)S(1)}, bf16[576,256]{1,0:T(8,128)(2,1)S(1)}, u32[]{:S(2)}, u32[]{:S(2)}) collective-permute-start(bf16[576,256]{1,0:T(8,128)(2,1)S(1)} %bitcast.88), channel_id=1, source_target_pairs={{0,120},{8,0},{16,8},{24,16},{32,24},{40,32},{48,40},{56,48},{64,5... | collective-permute-start | bytes 884744 | tf_op jit(solution)/shard_map/ppermute | solution.py:74
  591.4 10.4 %collective-permute-start.2 = (bf16[576,256]{1,0:T(8,128)(2,1)S(1)}, bf16[576,256]{1,0:T(8,128)(2,1)S(1)}, u32[]{:S(2)}, u32[]{:S(2)}) collective-permute-start(bf16[576,256]{1,0:T(8,128)(2,1)S(1)} %collective-permute-done), channel_id=1, source_target_pairs={{0,8},{8,16},{16,24},{24,32},{32,40},{40,48},{48,56},{56,64},{64,7... | collective-permute-start | bytes 884744 | tf_op jit(solution)/shard_map/ppermute | solution.py:69
  591.4 10.4 %collective-permute-start.3 = (bf16[576,256]{1,0:T(8,128)(2,1)S(1)}, bf16[576,256]{1,0:T(8,128)(2,1)S(1)}, u32[]{:S(2)}, u32[]{:S(2)}) collective-permute-start(bf16[576,256]{1,0:T(8,128)(2,1)S(1)} %collective-permute-done.1), channel_id=1, source_target_pairs={{0,120},{8,0},{16,8},{24,16},{32,24},{40,32},{48,40},{56,48},{64,5... | collective-permute-start | bytes 884744 | tf_op jit(solution)/shard_map/ppermute | solution.py:74
  601.8 17.3 %collective-permute-start.4 = (bf16[576,256]{1,0:T(8,128)(2,1)S(1)}, bf16[576,256]{1,0:T(8,128)(2,1)S(1)}, u32[]{:S(2)}, u32[]{:S(2)}) collective-permute-start(bf16[576,256]{1,0:T(8,128)(2,1)S(1)} %collective-permute-done.2), channel_id=1, source_target_pairs={{0,8},{8,16},{16,24},{24,32},{32,40},{40,48},{48,56},{56,64},{64,7... | collective-permute-start | bytes 884744 | tf_op jit(solution)/shard_map/ppermute | solution.py:69
  601.8 17.7 %collective-permute-start.5 = (bf16[576,256]{1,0:T(8,128)(2,1)S(1)}, bf16[576,256]{1,0:T(8,128)(2,1)S(1)}, u32[]{:S(2)}, u32[]{:S(2)}) collective-permute-start(bf16[576,256]{1,0:T(8,128)(2,1)S(1)} %collective-permute-done.3), channel_id=1, source_target_pairs={{0,120},{8,0},{16,8},{24,16},{32,24},{40,32},{48,40},{56,48},{64,5... | collective-permute-start | bytes 884744 | tf_op jit(solution)/shard_map/ppermute | solution.py:74
  619.1 8.9 %collective-permute-start.6 = (bf16[576,256]{1,0:T(8,128)(2,1)S(1)}, bf16[576,256]{1,0:T(8,128)(2,1)S(1)}, u32[]{:S(2)}, u32[]{:S(2)}) collective-permute-start(bf16[576,256]{1,0:T(8,128)(2,1)S(1)} %collective-permute-done.4), channel_id=1, source_target_pairs={{0,8},{8,16},{16,24},{24,32},{32,40},{40,48},{48,56},{56,64},{64,7... | collective-permute-start | bytes 884744 | tf_op jit(solution)/shard_map/ppermute | solution.py:69
  619.5 8.5 %collective-permute-start.7 = (bf16[576,256]{1,0:T(8,128)(2,1)S(1)}, bf16[576,256]{1,0:T(8,128)(2,1)S(1)}, u32[]{:S(2)}, u32[]{:S(2)}) collective-permute-start(bf16[576,256]{1,0:T(8,128)(2,1)S(1)} %collective-permute-done.5), channel_id=1, source_target_pairs={{0,120},{8,0},{16,8},{24,16},{32,24},{40,32},{48,40},{56,48},{64,5... | collective-permute-start | bytes 884744 | tf_op jit(solution)/shard_map/ppermute | solution.py:74
  628.0 8.9 %collective-permute-start.8 = (bf16[576,256]{1,0:T(8,128)(2,1)S(1)}, bf16[576,256]{1,0:T(8,128)(2,1)S(1)}, u32[]{:S(2)}, u32[]{:S(2)}) collective-permute-start(bf16[576,256]{1,0:T(8,128)(2,1)S(1)} %collective-permute-done.6), channel_id=1, source_target_pairs={{0,8},{8,16},{16,24},{24,32},{32,40},{40,48},{48,56},{56,64},{64,7... | collective-permute-start | bytes 884744 | tf_op jit(solution)/shard_map/ppermute | solution.py:69
  628.1 8.9 %collective-permute-start.9 = (bf16[576,256]{1,0:T(8,128)(2,1)S(1)}, bf16[576,256]{1,0:T(8,128)(2,1)S(1)}, u32[]{:S(2)}, u32[]{:S(2)}) collective-permute-start(bf16[576,256]{1,0:T(8,128)(2,1)S(1)} %collective-permute-done.7), channel_id=1, source_target_pairs={{0,120},{8,0},{16,8},{24,16},{32,24},{40,32},{48,40},{56,48},{64,5... | collective-permute-start | bytes 884744 | tf_op jit(solution)/shard_map/ppermute | solution.py:74
  636.9 8.9 %collective-permute-start.10 = (bf16[576,256]{1,0:T(8,128)(2,1)S(1)}, bf16[576,256]{1,0:T(8,128)(2,1)S(1)}, u32[]{:S(2)}, u32[]{:S(2)}) collective-permute-start(bf16[576,256]{1,0:T(8,128)(2,1)S(1)} %collective-permute-done.8), channel_id=1, source_target_pairs={{0,8},{8,16},{16,24},{24,32},{32,40},{40,48},{48,56},{56,64},{64,7... | collective-permute-start | bytes 884744 | tf_op jit(solution)/shard_map/ppermute | solution.py:69
  637.0 8.9 %collective-permute-start.11 = (bf16[576,256]{1,0:T(8,128)(2,1)S(1)}, bf16[576,256]{1,0:T(8,128)(2,1)S(1)}, u32[]{:S(2)}, u32[]{:S(2)}) collective-permute-start(bf16[576,256]{1,0:T(8,128)(2,1)S(1)} %collective-permute-done.9), channel_id=1, source_target_pairs={{0,120},{8,0},{16,8},{24,16},{32,24},{40,32},{48,40},{56,48},{64,5... | collective-permute-start | bytes 884744 | tf_op jit(solution)/shard_map/ppermute | solution.py:74
  645.8 8.9 %collective-permute-start.12 = (bf16[576,256]{1,0:T(8,128)(2,1)S(1)}, bf16[576,256]{1,0:T(8,128)(2,1)S(1)}, u32[]{:S(2)}, u32[]{:S(2)}) collective-permute-start(bf16[576,256]{1,0:T(8,128)(2,1)S(1)} %collective-permute-done.10), channel_id=1, source_target_pairs={{0,8},{8,16},{16,24},{24,32},{32,40},{40,48},{48,56},{56,64},{64,7... | collective-permute-start | bytes 884744 | tf_op jit(solution)/shard_map/ppermute | solution.py:69
  645.9 9.1 %collective-permute-start.13 = (bf16[576,256]{1,0:T(8,128)(2,1)S(1)}, bf16[576,256]{1,0:T(8,128)(2,1)S(1)}, u32[]{:S(2)}, u32[]{:S(2)}) collective-permute-start(bf16[576,256]{1,0:T(8,128)(2,1)S(1)} %collective-permute-done.11), channel_id=1, source_target_pairs={{0,120},{8,0},{16,8},{24,16},{32,24},{40,32},{48,40},{56,48},{64,5... | collective-permute-start | bytes 884744 | tf_op jit(solution)/shard_map/ppermute | solution.py:74
  651.1 15.8 %copy-start.1 = (f32[12,32,256]{2,1,0:T(8,128)S(1)}, f32[12,32,256]{2,1,0:T(8,128)}, u32[]{:S(2)}) copy-start(f32[12,32,256]{2,1,0:T(8,128)} %param.7) | copy-start | bytes 1179652
  654.7 10.0 %collective-permute-start.14 = (bf16[576,256]{1,0:T(8,128)(2,1)S(1)}, bf16[576,256]{1,0:T(8,128)(2,1)S(1)}, u32[]{:S(2)}, u32[]{:S(2)}) collective-permute-start(bf16[576,256]{1,0:T(8,128)(2,1)S(1)} %collective-permute-done.12), channel_id=1, source_target_pairs={{0,8},{8,16},{16,24},{24,32},{32,40},{40,48},{48,56},{56,64},{64,7... | collective-permute-start | bytes 884744 | tf_op jit(solution)/shard_map/ppermute | solution.py:69
  664.7 2.2 copy-start.5
Sparse Core Ops, SparseCore 0:
  23.2 150.8 all-reduce.4
  195.6 81.2 all-reduce.6
  291.7 148.1 all-reduce.8
  461.1 81.3 all-reduce.10
